TPU v7x, 32 devices: a whole 2x2x4 slice. The times are simulated.
32 devices in a mesh: row: 4 (over z), col: 8 (over y, x, core).
Axes of the slice: x: 2, y: 2, z: 4, core: 2. Of those that a mesh axis runs over, the one named last changes fastest.
Arguments:
- dec_src: float32 [2304, 8192], P('col', 'row'), may hold values from -6 to 6
- enc_tgt: float32 [2304, 16384], P('row', 'col'), may hold values from -0.125 to 0.125
- src_coacts: float32 [512, 8192], P('col', 'row'), may hold values from -6 to 6
- tgt_coacts: float32 [512, 16384], P('row', 'col'), may hold values from -6 to 6
- eval_src: float32 [512, 8192], P('col', 'row'), may hold values from -6 to 6
- enc_bias: float32 [16384], P('col'), may hold values from -0.5 to 0.5
- dec_tgt: float32 [2304, 16384], P('row', 'col'), may hold values from -0.046875 to 0.046875
- tile_mask: int32 [128, 256], P('row', 'col'), may hold values from 0 to 1, as said below
Outputs:
- recon: float32 [512, 2304], P('col', 'row')
Inputs may be any that keep to these rules, and one draw needn't show every extreme that they name: `tile_mask`: 1 keeps a tile, 0 prunes it; the share of kept tiles differs between regions of the grid.
All inputs are finite; a program needn't handle non-finite values.
Results may differ from a plain program's by a relative error of at most 0.0003.
Values sent between devices are 32-bit elements; how exact they have to be, the bound alone decides.
A program may use at most 192 MiB of HBM per device.

v0:
```python
import jax
import jax.numpy as jnp
from jax import lax
from jax.sharding import PartitionSpec as P

S = 8192
TILE = 64
PRECISE = lax.Precision.HIGHEST


def contract_first(left, right):
    return lax.dot_general(
        left, right, (((0,), (0,)), ((), ())), precision=PRECISE, preferred_element_type=jnp.float32
    )


def local(dec_src, enc_tgt, src_coacts, tgt_coacts, eval_src, enc_bias, dec_tgt, tile_mask):
    src_count = dec_src.shape[1]
    tgt_count = enc_tgt.shape[1]
    enc_full = lax.all_gather(enc_tgt, "row", axis=0, tiled=True)
    src_full, eval_full = (
        lax.all_gather(src_coacts, "col", axis=0, tiled=True),
        lax.all_gather(eval_src, "col", axis=0, tiled=True),
    )
    virtual = contract_first(lax.all_gather(dec_src, "col", axis=0, tiled=True), enc_full)
    coact = contract_first(src_full, lax.all_gather(tgt_coacts, "row", axis=0, tiled=True))
    coact = coact * (1.0 / jnp.sqrt(jnp.float32(src_full.shape[0])))
    tile_rows, tile_cols = tile_mask.shape
    mask_float = tile_mask.astype(jnp.float32)
    weighted = (
        (virtual * coact).reshape(tile_rows, TILE, tile_cols, TILE) * mask_float[:, None, :, None]
    ).reshape(src_count, tgt_count)
    partial_pre = jnp.dot(
        eval_full, weighted, precision=PRECISE, preferred_element_type=jnp.float32
    )
    scale = 1.0 / jnp.sqrt(jnp.float32(S))
    pre_acts = lax.psum(partial_pre, "row")
    hidden = jnp.maximum(pre_acts * scale + enc_bias[None, :], 0.0)
    recon_part = lax.dot_general(
        hidden,
        dec_tgt,
        (((1,), (1,)), ((), ())),
        precision=PRECISE,
        preferred_element_type=jnp.float32,
    )
    return lax.psum_scatter(recon_part, "col", scatter_dimension=0, tiled=True)


def solution(mesh):
    return jax.shard_map(
        local,
        mesh=mesh,
        in_specs=(
            P("col", "row"),
            P("row", "col"),
            P("col", "row"),
            P("row", "col"),
            P("col", "row"),
            P("col"),
            P("row", "col"),
            P("row", "col"),
        ),
        out_specs=P("col", "row"),
        check_vma=False,
    )
```

profile of v0, /device:TPU:0, one launch (start us, length us, event | category | flops | bytes accessed | tf_op | source)
XLA Modules:
  0.0 963.4 jit_solution(13110801990855593298)
XLA Ops:
  6.5 0.7 all-gather.12.cloned.1.call-update
  7.3 0.0 all-gather.10.cloned.1.call-start
  7.3 0.7 all-gather.10.cloned.1.call-update
  8.0 0.0 all-gather.8.cloned.1.call-start
  8.1 0.7 all-gather.8.cloned.1.call-update
  8.7 0.0 all-gather.6.cloned.1.call-start
  8.8 0.5 all-gather.6.cloned.1.call-update
  9.3 0.0 all-gather.14.cloned.1.call-start
  9.4 0.5 all-gather.14.cloned.1.call-update
  9.9 0.0 all-reduce.2.cloned.1.call-start
  10.0 11.9 %mul.29 = f32[32,64,32,64]{3,2,1,0:T(8,128)} broadcast(f32[32,32]{1,0:T(8,128)S(1)} %convert_element_type.3), dimensions={0,2} | broadcast | bytes 16781312 | tf_op jit(solution)/shard_map/mul | solution.py:31
  21.9 29.0 %mul.30 = f32[2048,2048]{1,0:T(8,128)} reshape(f32[32,64,32,64]{3,2,1,0:T(8,128)} %mul.29) | data formatting | bytes 33554432 | tf_op jit(solution)/shard_map/mul | solution.py:31
  50.9 41.5 %all-gather.12.cloned.1.call-done = f32[512,2048]{1,0:T(8,128)} async-done(((f32[128,2048]{1,0:T(8,128)}), f32[512,2048]{1,0:T(8,128)}) %all-gather.12.cloned.1.call-update) | async-done | bytes 4194320 | tf_op jit(solution)/shard_map/all_gather | solution.py:26
  92.4 37.0 %all-gather.10.cloned.1.call-done = f32[512,2048]{1,0:T(8,128)} async-done(((f32[64,2048]{1,0:T(8,128)}), f32[512,2048]{1,0:T(8,128)}) %all-gather.10.cloned.1.call-update) | async-done | bytes 4194320 | tf_op jit(solution)/shard_map/all_gather | solution.py:22
  129.4 31.4 %fusion.19 = f32[2048,2048]{1,0:T(8,128)} fusion(f32[512,2048]{1,0:T(8,128)} %all-gather.10.cloned.1.call-done, f32[512,2048]{1,0:T(8,128)} %all-gather.12.cloned.1.call-done), kind=kOutput, calls=%fused_computation.17 | convolution fusion | flops 25769803776 | bytes 25165824 | tf_op jit(solution)/shard_map/dot_general | solution.py:12
  160.8 292.8 %all-gather.8.cloned.1.call-done = f32[2304,2048]{1,0:T(8,128)} async-done(((f32[576,2048]{1,0:T(8,128)}), f32[2304,2048]{1,0:T(8,128)}) %all-gather.8.cloned.1.call-update) | async-done | bytes 18874384 | tf_op jit(solution)/shard_map/all_gather | solution.py:20
  453.6 99.2 %all-gather.6.cloned.1.call-done = f32[2304,2048]{1,0:T(8,128)} async-done(((f32[288,2048]{1,0:T(8,128)}), f32[2304,2048]{1,0:T(8,128)}) %all-gather.6.cloned.1.call-update) | async-done | bytes 18874384 | tf_op jit(solution)/shard_map/all_gather | solution.py:25
  552.8 125.5 %fusion.18 = f32[2048,2048]{1,0:T(8,128)} fusion(f32[2304,2048]{1,0:T(8,128)} %all-gather.6.cloned.1.call-done, f32[2304,2048]{1,0:T(8,128)} %all-gather.8.cloned.1.call-done), kind=kOutput, calls=%fused_computation.16 | convolution fusion | flops 115964116992 | bytes 54525952 | tf_op jit(solution)/shard_map/dot_general | solution.py:12
  678.3 0.0 all-gather.14.cloned.1.call-done
  678.4 62.9 %fusion.9 = f32[512,2048]{0,1:T(8,128)} fusion(f32[512,2048]{1,0:T(8,128)} %all-gather.14.cloned.1.call-done, f32[2048,2048]{1,0:T(8,128)} %mul.30, f32[2048,2048]{1,0:T(8,128)} %fusion.18, f32[2048,2048]{1,0:T(8,128)} %fusion.19), kind=kOutput, calls=%fused_computation.9 | convolution fusion | flops 25782386688 | bytes 58720256 | tf_op jit(solution)/shard_map/dot_general | solution.py:33
  741.3 0.0 reduce-scatter.2.cloned.1.call-start
  741.3 155.1 %all-reduce.2.cloned.1.call-done = f32[512,2048]{0,1:T(8,128)} async-done(((f32[512,2048]{0,1:T(8,128)}), f32[512,2048]{0,1:T(8,128)}) %all-reduce.2.cloned.1.call-update) | async-done | bytes 4194320 | tf_op jit(solution)/shard_map/psum | solution.py:37
  896.4 23.6 %fusion.5 = f32[512,576]{1,0:T(8,128)} fusion(f32[576,2048]{1,0:T(8,128)} %param.14, f32[512,2048]{0,1:T(8,128)} %all-reduce.2.cloned.1.call-done, f32[2048]{0:T(1024)S(1)} %copy-done.1), kind=kOutput, calls=%fused_computation.5 | convolution fusion | flops 7250903040 | bytes 10100736 | tf_op jit(solution)/shard_map/dot_general | solution.py:39
  920.1 36.3 %reduce-scatter.2.cloned.1.call-done = f32[64,576]{1,0:T(8,128)} async-done(((f32[512,576]{1,0:T(8,128)}), f32[64,576]{1,0:T(8,128)}) %reduce-scatter.2.cloned.1.call-update) | async-done | bytes 147472 | tf_op jit(solution)/shard_map/reduce_scatter | solution.py:46
  (8 shorter events, 0.0 us)
Async XLA Ops:
  6.5 3.4 copy-start
  6.5 85.9 %all-gather.12.cloned.1.call-start = ((), (), s32[]{:S(2)}) async-start(), calls=%async_computation.4 | async-start | bytes 5242880 | tf_op jit(solution)/shard_map/all_gather | solution.py:26
  7.3 122.1 %all-gather.10.cloned.1.call-start = ((), (), s32[]{:S(2)}) async-start(), calls=%async_computation.3 | async-start | bytes 4718592 | tf_op jit(solution)/shard_map/all_gather | solution.py:22
  8.0 445.6 %all-gather.8.cloned.1.call-start = ((), (), s32[]{:S(2)}) async-start(), calls=%async_computation.2 | async-start | bytes 23592960 | tf_op jit(solution)/shard_map/all_gather | solution.py:20
  8.7 544.0 %all-gather.6.cloned.1.call-start = ((), (), s32[]{:S(2)}) async-start(), calls=%async_computation.1 | async-start | bytes 21233664 | tf_op jit(solution)/shard_map/all_gather | solution.py:25
  9.3 669.0 %all-gather.14.cloned.1.call-start = ((), (), s32[]{:S(2)}) async-start(), calls=%async_computation.5 | async-start | bytes 4718592 | tf_op jit(solution)/shard_map/all_gather | solution.py:23
  9.9 886.5 %all-reduce.2.cloned.1.call-start = ((), (), s32[]{:S(2)}) async-start(), calls=%async_computation.6 | async-start | bytes 8388608 | tf_op jit(solution)/shard_map/psum | solution.py:37
  678.3 218.1 %copy-start.1 = (f32[2048]{0:T(1024)S(1)}, f32[2048]{0:T(1024)}, u32[]{:S(2)}) copy-start(f32[2048]{0:T(1024)} %param.13) | copy-start | bytes 24580
  741.3 215.1 %reduce-scatter.2.cloned.1.call-start = ((), (), s32[]{:S(2)}) async-start(), calls=%async_computation.7 | async-start | bytes 1474560 | tf_op jit(solution)/shard_map/reduce_scatter | solution.py:46
Sparse Core Ops, SparseCore 0:
  8.9 83.4 all-gather.11
  94.3 35.0 all-gather.9
  131.0 322.5 all-gather.7
  455.3 97.4 all-gather.5
  554.5 36.5 all-gather.13
  741.4 154.9 all-reduce.1
  920.2 36.1 reduce-scatter.1
where the time goes:
time: 970 us; the launch traced here: 963 us
  waiting for transfers between devices  665 us (69%)
  matrix products  243 us (25%)
  local copies, waits for them, and re-layouts  40.9 us (4%)
  between operations  13.7 us (1%)
    all_gather x1, waiting for transfers between devices, local(): enc_full = lax.all_gather(enc_tgt, 'row', axis=0, tiled=True)  293 us
    dot_general x2, matrix products, contract_first(): lax.dot_general(left, right, (((0,), (0,)), ((), ())), precision=PRECISE,...  157 us
    psum x1, waiting for transfers between devices, local(): pre_acts = lax.psum(partial_pre, 'row')  155 us
    all_gather x1, waiting for transfers between devices, local(): lax.all_gather(dec_src, 'col', axis=0, tiled=True)  99.2 us
    dot_general x1, matrix products, local(): jnp.dot(eval_full, weighted, precision=PRECISE, preferred_element_type=jn...  62.9 us
    all_gather x1, waiting for transfers between devices, local(): lax.all_gather(tgt_coacts, 'row', axis=0, tiled=True)  41.5 us
    mul x2, local copies, waits for them, and re-layouts, local(): (virtual * coact).reshape(tile_rows, TILE, tile_cols, TILE)  40.9 us
    all_gather x1, waiting for transfers between devices, local(): lax.all_gather(src_coacts, 'col', axis=0, tiled=True)  37 us
  transfers between devices with their start and end apart: 7, of which 6 were waited for; matrix products, arithmetic and copies ran while one was open for 21% of the time, Pallas kernels for 0%

commit v1 on v0

--- a/solution.py
+++ b/solution.py
@@ -17,7 +17,17 @@
 def local(dec_src, enc_tgt, src_coacts, tgt_coacts, eval_src, enc_bias, dec_tgt, tile_mask):
     src_count = dec_src.shape[1]
     tgt_count = enc_tgt.shape[1]
-    enc_full = lax.all_gather(enc_tgt, "row", axis=0, tiled=True)
+    n_axis = lax.psum(1, "row")
+    local_next = enc_tgt
+    by_rank = [local_next]
+    t = 0
+    last = [(it - 1, it) for it in range(1, n_axis)] + [(n_axis - 1, 0)]
+    while t < n_axis - 1:
+        local_next = lax.ppermute(local_next, "row", last)
+        by_rank += [local_next]
+        t += 1
+    m_next = jnp.concatenate([*reversed(by_rank)], 0)
+    enc_full = jnp.roll(m_next, (lax.axis_index("row") + 1) * local_next.shape[0], 0)
     src_full, eval_full = (
         lax.all_gather(src_coacts, "col", axis=0, tiled=True),
         lax.all_gather(eval_src, "col", axis=0, tiled=True),

time: 970 us -> 822 us (0.85)
  waiting for transfers between devices: 665 us -> 500 us
  local copies, waits for them, and re-layouts: 40.9 us -> 76 us
  matrix products: 243 us -> 220 us
    ppermute x0 -> x3, waiting for transfers between devices: none -> 308 us  [local(): local_next = lax.ppermute(local_next, 'row', last)]
    all_gather x1 -> x0, waiting for transfers between devices: 293 us -> none  [local(): enc_full = lax.all_gather(enc_tgt, 'row', axis=0, tiled=True)]
    all_gather x1, waiting for transfers between devices: 99.2 us -> 0.01 us  [local(): lax.all_gather(dec_src, 'col', axis=0, tiled=True)]
    all_gather x1, waiting for transfers between devices: 41.5 us -> 0.01 us  [local(): lax.all_gather(tgt_coacts, 'row', axis=0, tiled=True)]
    all_gather x1, waiting for transfers between devices: 37 us -> 0.01 us  [local(): lax.all_gather(src_coacts, 'col', axis=0, tiled=True)]
    unnamed x4 -> x19, local copies, waits for them, and re-layouts: 0.01 us -> 33.3 us
    dot_general x1, matrix products: 62.9 us -> 37.9 us  [local(): jnp.dot(eval_full, weighted, precision=PRECISE, preferred_element_type=jn...]
  transfers between devices with their start and end apart: 7 -> 9, of which waited for: 6 -> 5; matrix products, arithmetic and copies ran while one was open for 21% -> 29% of each run, Pallas kernels for 0% -> 0%
where the time goes in v1:
time: 822 us; the launch traced here: 813 us
  waiting for transfers between devices  500 us (61%)
  matrix products  220 us (27%)
  local copies, waits for them, and re-layouts  76 us (9%)
  between operations  13.9 us (2%)
    ppermute x3, waiting for transfers between devices, local(): local_next = lax.ppermute(local_next, 'row', last)  308 us
    dot_general x2, matrix products, contract_first(): lax.dot_general(left, right, (((0,), (0,)), ((), ())), precision=PRECISE,...  158 us
    psum x1, waiting for transfers between devices, local(): pre_acts = lax.psum(partial_pre, 'row')  153 us
    mul x2, local copies, waits for them, and re-layouts, local(): (virtual * coact).reshape(tile_rows, TILE, tile_cols, TILE)  39.8 us
    dot_general x1, matrix products, local(): jnp.dot(eval_full, weighted, precision=PRECISE, preferred_element_type=jn...  37.9 us
    reduce_scatter x1, waiting for transfers between devices, local(): return lax.psum_scatter(recon_part, 'col', scatter_dimension=0, tiled=True)  36.3 us
    unnamed x19, local copies, waits for them, and re-layouts  33.3 us
    dot_general x1, matrix products, local(): lax.dot_general(hidden, dec_tgt, (((1,), (1,)), ((), ())), precision=PREC...  23.6 us
  transfers between devices with their start and end apart: 9, of which 5 were waited for; matrix products, arithmetic and copies ran while one was open for 29% of the time, Pallas kernels for 0%

profile of v1, /device:TPU:0, one launch (start us, length us, event | category | flops | bytes accessed | tf_op | source)
XLA Modules:
  0.0 813.2 jit_solution(17789372261125082259)
XLA Ops:
  6.5 0.7 all-gather.9.cloned.1.call-update
  7.3 0.7 all-gather.7.cloned.1.call-update
  8.8 3.1 collective-permute-start
  11.9 171.5 %collective-permute-done = f32[576,2048]{1,0:T(8,128)S(1)} collective-permute-done((f32[576,2048]{1,0:T(8,128)}, f32[576,2048]{1,0:T(8,128)S(1)}, u32[]{:S(2)}, u32[]{:S(2)}) %collective-permute-start) | collective-permute-done | bytes 4718624 | tf_op jit(solution)/shard_map/ppermute | solution.py:26
  183.4 2.1 copy-done
  185.6 104.9 %collective-permute-done.1 = f32[576,2048]{1,0:T(8,128)} collective-permute-done((f32[576,2048]{1,0:T(8,128)S(1)}, f32[576,2048]{1,0:T(8,128)}, u32[]{:S(2)}, u32[]{:S(2)}) %collective-permute-start.1) | collective-permute-done | bytes 4718624 | tf_op jit(solution)/shard_map/ppermute | solution.py:26
  290.6 0.7 convert_element_type.3
  291.4 11.4 %mul.33 = f32[32,64,32,64]{1,0,3,2:T(8,128)} broadcast(f32[32,32]{0,1:T(8,128)S(1)} %copy.9), dimensions={0,2} | broadcast | bytes 16781312 | tf_op jit(solution)/shard_map/mul | solution.py:41
  302.7 28.4 %mul.34 = f32[2048,2048]{0,1:T(8,128)} reshape(f32[32,64,32,64]{1,0,3,2:T(8,128)} %mul.33) | data formatting | bytes 33554432 | tf_op jit(solution)/shard_map/mul | solution.py:41
  331.1 31.7 %fusion.21 = f32[2048,2048]{0,1:T(8,128)} fusion(f32[512,2048]{1,0:T(8,128)} %all-gather.7.cloned.1.call-done, f32[512,2048]{1,0:T(8,128)} %all-gather.9.cloned.1.call-done), kind=kOutput, calls=%fused_computation.27 | convolution fusion | flops 25769803776 | bytes 25165824 | tf_op jit(solution)/shard_map/dot_general | solution.py:12
  362.9 31.8 %collective-permute-done.2 = f32[576,2048]{1,0:T(8,128)} collective-permute-done((f32[576,2048]{1,0:T(8,128)}, f32[576,2048]{1,0:T(8,128)}, u32[]{:S(2)}, u32[]{:S(2)}) %collective-permute-start.2) | collective-permute-done | bytes 4718624 | tf_op jit(solution)/shard_map/ppermute | solution.py:26
  394.7 5.1 constant_dynamic-update-slice_fusion.7
  399.7 5.2 constant_dynamic-update-slice_fusion.6
  404.9 5.3 constant_dynamic-update-slice_fusion.5
  410.2 2.7 constant_dynamic-update-slice_fusion.4
  412.9 5.2 constant_dynamic-update-slice_fusion.3
  418.1 5.1 constant_dynamic-update-slice_fusion.2
  423.2 2.7 constant_dynamic-update-slice_fusion.1
  425.8 2.8 constant_dynamic-update-slice_fusion
  428.7 126.5 %fusion = f32[2048,2048]{1,0:T(8,128)} fusion(f32[2304,2048]{1,0:T(8,128)} %all-gather.5.cloned.1.call-done, f32[4608,2048]{1,0:T(8,128)} %constant_dynamic-update-slice_fusion, s32[]{:T(128)S(6)} %select_n.14), kind=kOutput, calls=%fused_computation | convolution fusion | flops 115964116992 | bytes 54525956 | tf_op jit(solution)/shard_map/dot_general | solution.py:12
  555.2 37.9 %fusion.11 = f32[512,2048]{0,1:T(8,128)} fusion(f32[512,2048]{1,0:T(8,128)} %all-gather.11.cloned.1.call-done, f32[2048,2048]{0,1:T(8,128)} %mul.34, f32[2048,2048]{1,0:T(8,128)} %fusion, f32[2048,2048]{0,1:T(8,128)} %fusion.21), kind=kOutput, calls=%fused_computation.11 | convolution fusion | flops 25782386688 | bytes 58720256 | tf_op jit(solution)/shard_map/dot_general | solution.py:43
  593.2 152.9 %all-reduce.2.cloned.1.call-done = f32[512,2048]{0,1:T(8,128)} async-done(((f32[512,2048]{0,1:T(8,128)}), f32[512,2048]{0,1:T(8,128)}) %all-reduce.2.cloned.1.call-update) | async-done | bytes 4194320 | tf_op jit(solution)/shard_map/psum | solution.py:47
  746.0 23.6 %fusion.7 = f32[512,576]{1,0:T(8,128)} fusion(f32[576,2048]{1,0:T(8,128)} %param.14, f32[512,2048]{0,1:T(8,128)} %all-reduce.2.cloned.1.call-done, f32[2048]{0:T(1024)S(1)} %copy-done.1), kind=kOutput, calls=%fused_computation.7 | convolution fusion | flops 7250903040 | bytes 10100736 | tf_op jit(solution)/shard_map/dot_general | solution.py:49
  769.7 36.3 %reduce-scatter.2.cloned.1.call-done = f32[64,576]{1,0:T(8,128)} async-done(((f32[512,576]{1,0:T(8,128)}), f32[64,576]{1,0:T(8,128)}) %reduce-scatter.2.cloned.1.call-update) | async-done | bytes 147472 | tf_op jit(solution)/shard_map/reduce_scatter | solution.py:56
  (30 shorter events, 1.1 us)
Async XLA Ops:
  6.5 324.6 %all-gather.9.cloned.1.call-start = ((), (), s32[]{:S(2)}) async-start(), calls=%async_computation.3 | async-start | bytes 5242880 | tf_op jit(solution)/shard_map/all_gather | solution.py:36
  7.3 323.9 %all-gather.7.cloned.1.call-start = ((), (), s32[]{:S(2)}) async-start(), calls=%async_computation.2 | async-start | bytes 4718592 | tf_op jit(solution)/shard_map/all_gather | solution.py:32
  8.0 420.6 %all-gather.5.cloned.1.call-start = ((), (), s32[]{:S(2)}) async-start(), calls=%async_computation.1 | async-start | bytes 21233664 | tf_op jit(solution)/shard_map/all_gather | solution.py:35
  8.7 546.5 %all-gather.11.cloned.1.call-start = ((), (), s32[]{:S(2)}) async-start(), calls=%async_computation.4 | async-start | bytes 4718592 | tf_op jit(solution)/shard_map/all_gather | solution.py:33
  8.8 174.6 %collective-permute-start = (f32[576,2048]{1,0:T(8,128)}, f32[576,2048]{1,0:T(8,128)S(1)}, u32[]{:S(2)}, u32[]{:S(2)}) collective-permute-start(f32[576,2048]{1,0:T(8,128)} %param.9), channel_id=1, source_target_pairs={{0,8},{8,16},{16,24},{24,0},{1,9},{9,17},{17,25},{25,1},{2,10},{10... | collective-permute-start | bytes 14155784 | tf_op jit(solution)/shard_map/ppermute | solution.py:26
  183.4 2.1 copy-start
  185.6 104.9 %collective-permute-start.1 = (f32[576,2048]{1,0:T(8,128)S(1)}, f32[576,2048]{1,0:T(8,128)}, u32[]{:S(2)}, u32[]{:S(2)}) collective-permute-start(f32[576,2048]{1,0:T(8,128)S(1)} %collective-permute-done), channel_id=1, source_target_pairs={{0,8},{8,16},{16,24},{24,0},{1,9},{9,17},{17,25},{25,1},{2,10},{10... | collective-permute-start | bytes 14155784 | tf_op jit(solution)/shard_map/ppermute | solution.py:26
  290.5 104.2 %collective-permute-start.2 = (f32[576,2048]{1,0:T(8,128)}, f32[576,2048]{1,0:T(8,128)}, u32[]{:S(2)}, u32[]{:S(2)}) collective-permute-start(f32[576,2048]{1,0:T(8,128)} %collective-permute-done.1), channel_id=1, source_target_pairs={{0,8},{8,16},{16,24},{24,0},{1,9},{9,17},{17,25},{25,1},{2,10},{10... | collective-permute-start | bytes 14155784 | tf_op jit(solution)/shard_map/ppermute | solution.py:26
  290.5 455.6 %all-reduce.2.cloned.1.call-start = ((), (), s32[]{:S(2)}) async-start(), calls=%async_computation.5 | async-start | bytes 8388608 | tf_op jit(solution)/shard_map/psum | solution.py:47
  362.9 47.3 %slice-start = ((s8[4718592]{0:T(1024)(128)(4,1)}), s8[4194304]{0:T(1024)(128)(4,1)S(1)}, s32[]{:S(2)}) async-start(s8[4718592]{0:T(1024)(128)(4,1)} %bitcast.19), calls=%async_computation.7 | async-start | bytes 8388608
  399.7 10.5 %slice-start.1 = ((s8[4718592]{0:T(1024)(128)(4,1)}), s8[524288]{0:T(1024)(128)(4,1)S(1)}, s32[]{:S(2)}) async-start(s8[4718592]{0:T(1024)(128)(4,1)} %bitcast.19), calls=%async_computation.8 | async-start | bytes 1048576
  404.9 18.3 %slice-start.2 = ((s8[4718592]{0:T(1024)(128)(4,1)}), s8[4194304]{0:T(1024)(128)(4,1)S(1)}, s32[]{:S(2)}) async-start(s8[4718592]{0:T(1024)(128)(4,1)} %bitcast.21), calls=%async_computation.9 | async-start | bytes 8388608
  412.9 10.3 %slice-start.3 = ((s8[4718592]{0:T(1024)(128)(4,1)}), s8[524288]{0:T(1024)(128)(4,1)S(1)}, s32[]{:S(2)}) async-start(s8[4718592]{0:T(1024)(128)(4,1)} %bitcast.21), calls=%async_computation.10 | async-start | bytes 1048576
  555.2 190.9 %copy-start.1 = (f32[2048]{0:T(1024)S(1)}, f32[2048]{0:T(1024)}, u32[]{:S(2)}) copy-start(f32[2048]{0:T(1024)} %param.13) | copy-start | bytes 24580
  593.1 212.9 %reduce-scatter.2.cloned.1.call-start = ((), (), s32[]{:S(2)}) async-start(), calls=%async_computation.6 | async-start | bytes 1474560 | tf_op jit(solution)/shard_map/reduce_scatter | solution.py:56
Sparse Core Ops, SparseCore 0:
  8.9 150.7 all-gather.8
  161.6 34.8 all-gather.6
  198.3 98.5 all-gather.4
  298.7 36.5 all-gather.10
  593.2 152.7 all-reduce.1
  769.8 36.1 reduce-scatter.1
